TPU v7x, 32 devices: a whole 2x2x4 slice. The times are simulated.
32 devices in a mesh: space: 8 (over y, x, core), members: 4 (over z).
Axes of the slice: x: 2, y: 2, z: 4, core: 2. Of those that a mesh axis runs over, the one named last changes fastest.
Arguments:
- ensemble: bfloat16 [128, 65536], P('members', 'space'), may hold values from -6 to 6
- op_blocks: bfloat16 [512, 3, 128, 128], P('space'), may hold values from -0.3125 to 0.3125
- col_index: int32 [512, 2], P('space'), may hold values from 0 to 511, as said below
- weights: float32 [128, 512], P('members', 'space')
- innovations: float32 [2, 65536], P(None, 'space'), may hold values from -6 to 6
- obs_precision: float32 [2, 65536], P(None, 'space'), may hold values from 0.25 to 4
Outputs:
- grad_ens: float32 [128, 65536], P('members', 'space')
- direction: float32 [128, 512], P('members', 'space')
Inputs may be any that keep to these rules, and one draw needn't show every extreme that they name: col_index[r, 0] lies in [r - 32, r - 1] and col_index[r, 1] in [r + 1, r + 32], each clipped to the grid; in every aligned run of 64 block-rows some row reaches back by exactly 32 and some row forward by exactly 32, before clipping.
All inputs are finite; a program needn't handle non-finite values.
Results may differ from a plain program's by a relative error of at most 0.011.
Values may be sent and summed in bfloat16 or wider, within the bound.
No kernel may reach another device: no remote copies, remote signals or barrier semaphores. Data moves between devices by JAX's collectives and lax.ppermute only.
A program may use at most 64 MiB of HBM per device.

v0:
```python
import jax
import jax.numpy as jnp
from jax import lax
from jax.sharding import PartitionSpec as P

MEMBERS = 128


def padded(x, sides, width):
    for axis, dim in sides:
        devices, length = (lax.axis_size(axis), x.shape[dim])
        up = [(i, (i + 1) % devices) for i in range(devices - 1)]
        down = [(j, i) for i, j in up]
        last = lax.slice_in_dim(x, length - width, length, axis=dim)
        leading = lax.slice_in_dim(x, 0, width, axis=dim)
        before = lax.ppermute(last, axis, up)
        after = lax.ppermute(leading, axis, down)
        x = jnp.concatenate([before, x, after], axis=dim)
    return x


def on_device(ensemble, op_blocks, col_index, weights, innovations, obs_precision):
    member_count = ensemble.shape[0]
    blocks = op_blocks.shape[0]
    per_row = op_blocks.shape[1]
    block_size = op_blocks.shape[2]
    offset_rows = lax.axis_index("space") * blocks - blocks
    local_cols = col_index - offset_rows
    own_rows = (jnp.arange(blocks, dtype=jnp.int32) + blocks)[:, None]
    every_col = jnp.concatenate([own_rows, local_cols], axis=1)
    wide_rows = blocks + 2 * blocks

    def widen_halo(flat_values):
        widened = padded(flat_values, (("space", 1),), blocks * block_size)
        return widened.reshape(member_count, wide_rows, block_size)

    def forward(values_in):
        flat_values = values_in.reshape(member_count, blocks * block_size)
        widened = widen_halo(flat_values)
        picked = widened[:, every_col, :]
        return jnp.einsum("rkij,mrkj->mri", op_blocks, picked, preferred_element_type=jnp.float32)

    def adjoint(cotangent):
        contributions = jnp.einsum(
            "rkij,mri->mrkj", op_blocks, cotangent, preferred_element_type=jnp.float32
        )
        spread_rows = jnp.zeros((member_count, wide_rows, block_size), jnp.float32)
        spread_rows = spread_rows.at[:, every_col.reshape(-1), :].add(
            contributions.reshape(member_count, blocks * per_row, block_size)
        )
        outer_rims = jnp.concatenate(
            [spread_rows[:, :blocks], spread_rows[:, blocks + blocks :]], axis=1
        )
        outer_rims = outer_rims.reshape(member_count, 2 * blocks * block_size)
        received = padded(outer_rims, (("space", 1),), blocks * block_size)
        received = received.reshape(member_count, 4 * blocks, block_size)
        own_sums = spread_rows[:, blocks : blocks + blocks]
        own_sums = own_sums.at[:, :blocks].add(received[:, :blocks])
        own_sums = own_sums.at[:, blocks - blocks :].add(received[:, 3 * blocks :])
        return own_sums

    states = ensemble.reshape(member_count, blocks, block_size)
    prop_one = forward(states).astype(jnp.bfloat16)
    prop_two = forward(prop_one).astype(jnp.bfloat16)
    member_scale = (MEMBERS - 1) ** (-0.5)
    weight_col = weights[:, :, None]
    partial_sums = jnp.stack(
        [
            jnp.sum(weight_col * prop_one.astype(jnp.float32), axis=0),
            jnp.sum(weight_col * prop_two.astype(jnp.float32), axis=0),
        ]
    )
    observed = innovations.reshape(2, blocks, block_size)
    precision = obs_precision.reshape(2, blocks, block_size)
    increments = lax.psum(partial_sums, "members") * member_scale
    residual = precision * (increments - observed)
    cot_one = (member_scale * weight_col * residual[0][None]).astype(jnp.bfloat16)
    cot_two = (member_scale * weight_col * residual[1][None]).astype(jnp.bfloat16)
    adjoint_mid = (cot_one.astype(jnp.float32) + adjoint(cot_two)).astype(jnp.bfloat16)
    grad_ens = adjoint(adjoint_mid).reshape(member_count, blocks * block_size)
    products = (
        prop_one.astype(jnp.float32) * residual[0][None]
        + prop_two.astype(jnp.float32) * residual[1][None]
    )
    grad_weights = weights + member_scale * jnp.sum(products, axis=2)
    squares = lax.psum(jnp.sum(grad_weights * grad_weights, axis=1), "space")
    mean_square = squares / (blocks * lax.axis_size("space"))
    direction = grad_weights / jnp.sqrt(mean_square + 1e-06)[:, None]
    return (grad_ens, direction)


def solution(mesh):
    placed = (
        P("members", "space"),
        P("space", None, None, None),
        P("space", None),
        P("members", "space"),
        P(None, "space"),
        P(None, "space"),
    )
    return jax.shard_map(
        on_device,
        mesh=mesh,
        in_specs=placed,
        out_specs=(P("members", "space"), P("members", "space")),
        check_vma=False,
    )
```

profile of v0, /device:TPU:1, one launch (start us, length us, event | category | flops | bytes accessed | tf_op | source)
XLA Modules:
  0.0 225.6 jit_solution(5958671020050633099)
XLA Ops:
  7.2 4.5 %collective-permute-start = (bf16[32,8192]{1,0:T(8,128)(2,1)}, bf16[32,8192]{1,0:T(8,128)(2,1)S(1)}, u32[]{:S(2)}, u32[]{:S(2)}) collective-permute-start(bf16[32,8192]{1,0:T(8,128)(2,1)} %param.22), channel_id=1, source_target_pairs={{0,4},{4,8},{8,12},{12,16},{16,20},{20,24},{24,28},{1,5},{5,9},{9,... | collective-permute-start | bytes 1572872 | tf_op jit(solution)/shard_map/ppermute | solution.py:16
  11.7 1.9 collective-permute-start.1
  13.7 0.7 fusion.36
  14.6 3.5 %collective-permute-done = bf16[32,8192]{1,0:T(8,128)(2,1)S(1)} collective-permute-done((bf16[32,8192]{1,0:T(8,128)(2,1)}, bf16[32,8192]{1,0:T(8,128)(2,1)S(1)}, u32[]{:S(2)}, u32[]{:S(2)}) %collective-permute-start) | collective-permute-done | bytes 524320 | tf_op jit(solution)/shard_map/ppermute | solution.py:16
  18.1 7.2 %collective-permute-done.1 = bf16[32,8192]{1,0:T(8,128)(2,1)S(1)} collective-permute-done((bf16[32,8192]{1,0:T(8,128)(2,1)}, bf16[32,8192]{1,0:T(8,128)(2,1)S(1)}, u32[]{:S(2)}, u32[]{:S(2)}) %collective-permute-start.1) | collective-permute-done | bytes 524320 | tf_op jit(solution)/shard_map/ppermute | solution.py:17
  25.3 1.3 copy_bitcast_fusion.2
  26.6 0.9 gather_fusion
  27.6 5.1 %fusion = bf16[64,32,128]{2,1,0:T(8,128)(2,1)S(1)} fusion(bf16[32,64,3,128]{3,0,2,1:T(8,128)(2,1)S(1)} %bitcast.123, bf16[64,3,128,128]{3,2,1,0:T(8,128)(2,1)} %param.23), kind=kOutput, calls=%fused_computation.17 | convolution fusion | flops 201588736 | bytes 8388608 | tf_op jit(solution)/shard_map/rkij,mrkj->mri/dot_general | solution.py:41
  32.7 1.9 collective-permute-start.3
  34.6 3.6 %collective-permute-start.2 = (bf16[32,8192]{1,0:T(8,128)(2,1)S(1)}, bf16[32,8192]{1,0:T(8,128)(2,1)S(1)}, u32[]{:S(2)}, u32[]{:S(2)}) collective-permute-start(bf16[32,8192]{1,0:T(8,128)(2,1)S(1)} %copy_bitcast_fusion.4), channel_id=1, source_target_pairs={{0,4},{4,8},{8,12},{12,16},{16,20},{20,24},{24,28},{1,5},{5,9},{9,... | collective-permute-start | bytes 1572872 | tf_op jit(solution)/shard_map/ppermute | solution.py:16
  38.6 6.4 %collective-permute-done.3 = bf16[32,8192]{1,0:T(8,128)(2,1)S(1)} collective-permute-done((bf16[32,8192]{1,0:T(8,128)(2,1)S(1)}, bf16[32,8192]{1,0:T(8,128)(2,1)S(1)}, u32[]{:S(2)}, u32[]{:S(2)}) %collective-permute-start.3) | collective-permute-done | bytes 524320 | tf_op jit(solution)/shard_map/ppermute | solution.py:17
  45.2 1.3 pad_maximum_fusion
  46.5 2.3 %gather_fusion.1 = bf16[192,32,128]{2,1,0:T(8,128)(2,1)S(1)} fusion(bf16[32,192,128]{2,0,1:T(8,128)(2,1)} %pad_maximum_fusion, s32[1024]{0:T(1024)S(1)} %pad_clamp_fusion), kind=kCustom, calls=%fused_computation.1 | custom fusion | bytes 3146496 | tf_op jit(solution)/shard_map/gather | solution.py:40
  48.9 5.1 %fusion.4 = (f32[64,128]{1,0:T(8,128)S(1)}, f32[64,128]{1,0:T(8,128)S(1)}, f32[32,64,128]{2,0,1:T(8,128)S(1)}) fusion(f32[32,64]{0,1:T(8,128)S(1)} %copy.44, bf16[64,32,128]{2,1,0:T(8,128)(2,1)S(1)} %fusion, bf16[32,64,3,128]{3,0,2,1:T(8,128)(2,1)S(1)} %bitcast.122, bf16[64,3,128,128]{3,2,1,0:T(8,128)(2,1)} %param.23), kind=kOutput, calls=%fused_computation.21 | convolution fusion | flops 203145216 | bytes 9510912 | tf_op jit(solution)/shard_map/rkij,mrkj->mri/dot_general | solution.py:41
  54.0 0.6 pad_maximum_fusion.1
  54.7 36.1 %all-reduce.2.cloned.1.call-done = f32[2,64,128]{2,1,0:T(8,128)} async-done(((f32[2,64,128]{2,1,0:T(8,128)}), f32[2,64,128]{2,1,0:T(8,128)}) %all-reduce.2.cloned.1.call-update) | async-done | bytes 65552 | tf_op jit(solution)/shard_map/psum | solution.py:75
  90.8 0.9 fusion.22
  91.7 0.4 fusion.6
  92.1 13.8 %psum.15 = f32[32]{0:T(128)S(1)} all-reduce(f32[32]{0:T(128)S(1)} %multiply_reduce_fusion.1), channel_id=1, replica_groups=mesh['space'=8,'members'=4] {'space'}, use_global_device_ids=true, to_apply=%region_7.0 | all-reduce | flops 32 | bytes 256 | tf_op jit(solution)/shard_map/psum | solution.py:86
  105.9 5.7 %fusion.13 = f32[64,32,3,128]{3,1,2,0:T(8,128)} fusion(bf16[64,3,128,128]{3,2,1,0:T(8,128)(2,1)} %param.23, f32[64,128]{1,0:T(8,128)S(1)} %get-tuple-element.99, f32[32,64]{0,1:T(8,128)S(1)} %get-tuple-element.101), kind=kOutput, calls=%fused_computation.36 | convolution fusion | flops 201850880 | bytes 9478144 | tf_op jit(solution)/shard_map/rkij,mri->mrkj/dot_general | solution.py:44
  111.6 0.4 broadcast.210.clone
  112.0 17.3 %scatter_fusion = f32[32,192,128]{2,0,1:T(8,128)S(1)} fusion(f32[32,192,128]{2,0,1:T(8,128)S(1)} %broadcast.210.clone, s32[192]{0:T(256)S(1)} %bitcast.128, f32[192,32,128]{2,1,0:T(8,128)} %bitcast.119), kind=kCustom, calls=%fused_computation.2 | custom fusion | flops 786432 | bytes 9437952 | tf_op jit(solution)/shard_map/scatter-add | solution.py:48
  129.3 0.2 fusion.27
  129.5 0.1 copy_bitcast_fusion.1
  129.8 1.9 collective-permute-start.4
  131.7 2.6 %collective-permute-start.5 = (f32[32,8192]{1,0:T(8,128)S(1)}, f32[32,8192]{1,0:T(8,128)S(1)}, u32[]{:S(2)}, u32[]{:S(2)}) collective-permute-start(f32[32,8192]{1,0:T(8,128)S(1)} %get-tuple-element.97), channel_id=1, source_target_pairs={{4,0},{8,4},{12,8},{16,12},{20,16},{24,20},{28,24},{5,1},{9,5},{13... | collective-permute-start | bytes 3145736 | tf_op jit(solution)/shard_map/ppermute | solution.py:17
  134.4 9.1 %collective-permute-done.4 = f32[32,8192]{1,0:T(8,128)S(1)} collective-permute-done((f32[32,8192]{1,0:T(8,128)S(1)}, f32[32,8192]{1,0:T(8,128)S(1)}, u32[]{:S(2)}, u32[]{:S(2)}) %collective-permute-start.4) | collective-permute-done | bytes 1048608 | tf_op jit(solution)/shard_map/ppermute | solution.py:16
  143.4 14.6 %collective-permute-done.5 = f32[32,8192]{1,0:T(8,128)S(1)} collective-permute-done((f32[32,8192]{1,0:T(8,128)S(1)}, f32[32,8192]{1,0:T(8,128)S(1)}, u32[]{:S(2)}, u32[]{:S(2)}) %collective-permute-start.5) | collective-permute-done | bytes 1048608 | tf_op jit(solution)/shard_map/ppermute | solution.py:17
  158.0 0.3 maximum_bitcast_fusion
  158.3 0.7 copy.78
  159.1 0.2 fusion.25
  159.3 0.4 slice-done
  159.6 1.3 slice-done.1
  160.9 3.9 %fusion.16 = f32[64,32,3,128]{3,1,2,0:T(8,128)} fusion(bf16[64,3,128,128]{3,2,1,0:T(8,128)(2,1)S(1)} %bitcast.116, f32[32,64,128]{2,1,0:T(8,128)S(1)} %get-tuple-element.89, f32[32,64,128]{2,1,0:T(8,128)S(1)} %get-tuple-element.88, f32[32,192,128]{2,0,1:T(8,128)S(1)} %scatter_fusion, f32[64,128]{1,0:T(8,128)S(1)} %get-tuple-element.98, ...), kind=kOutput, calls=%fused_computation.38 | convolution fusion | flops 203161600 | bytes 12648448 | tf_op jit(solution)/shard_map/rkij,mri->mrkj/dot_general | solution.py:44
  164.8 0.4 broadcast.210
  165.2 17.3 %scatter_fusion.1 = f32[32,192,128]{2,0,1:T(8,128)S(1)} fusion(f32[32,192,128]{2,0,1:T(8,128)S(1)} %broadcast.210, s32[192]{0:T(256)S(1)} %bitcast.129, f32[192,32,128]{2,1,0:T(8,128)} %bitcast.118), kind=kCustom, calls=%fused_computation.3 | custom fusion | flops 786432 | bytes 9437952 | tf_op jit(solution)/shard_map/scatter-add | solution.py:48
  182.5 0.2 fusion.26
  182.8 1.3 copy-done
  184.1 1.5 fusion.28
  185.6 1.9 collective-permute-start.6
  187.5 3.4 %collective-permute-start.7 = (f32[32,8192]{1,0:T(8,128)}, f32[32,8192]{1,0:T(8,128)}, u32[]{:S(2)}, u32[]{:S(2)}) collective-permute-start(f32[32,8192]{1,0:T(8,128)} %get-tuple-element.95), channel_id=1, source_target_pairs={{4,0},{8,4},{12,8},{16,12},{20,16},{24,20},{28,24},{5,1},{9,5},{13... | collective-permute-start | bytes 3145736 | tf_op jit(solution)/shard_map/ppermute | solution.py:17
  190.9 0.7 copy.60
  191.6 8.0 %collective-permute-done.6 = f32[32,8192]{1,0:T(8,128)} collective-permute-done((f32[32,8192]{1,0:T(8,128)}, f32[32,8192]{1,0:T(8,128)}, u32[]{:S(2)}, u32[]{:S(2)}) %collective-permute-start.6) | collective-permute-done | bytes 1048608 | tf_op jit(solution)/shard_map/ppermute | solution.py:16
  199.6 13.5 %collective-permute-done.7 = f32[32,8192]{1,0:T(8,128)} collective-permute-done((f32[32,8192]{1,0:T(8,128)}, f32[32,8192]{1,0:T(8,128)}, u32[]{:S(2)}, u32[]{:S(2)}) %collective-permute-start.7) | collective-permute-done | bytes 1048608 | tf_op jit(solution)/shard_map/ppermute | solution.py:17
  213.1 2.4 %maximum_bitcast_fusion.1 = f32[4,8,256,128]{3,1,2,0:T(8,128)S(1)} fusion(f32[32,8192]{1,0:T(8,128)} %collective-permute-done.7, f32[32,16384]{1,0:T(8,128)} %copy-done, f32[32,8192]{1,0:T(8,128)} %collective-permute-done.6), kind=kLoop, calls=%fused_computation.5 | loop fusion | flops 2097152 | bytes 8388608
  215.5 0.7 copy.79
  216.3 0.2 fusion.24
  216.5 2.2 copy_bitcast_fusion.3
  (36 shorter events, 1.3 us)
Async XLA Ops:
  7.2 83.7 %all-reduce.2.cloned.1.call-start = ((), (), s32[]{:S(2)}) async-start(), calls=%async_computation | async-start | bytes 131072 | tf_op jit(solution)/shard_map/psum | solution.py:75
  7.2 10.9 %collective-permute-start = (bf16[32,8192]{1,0:T(8,128)(2,1)}, bf16[32,8192]{1,0:T(8,128)(2,1)S(1)}, u32[]{:S(2)}, u32[]{:S(2)}) collective-permute-start(bf16[32,8192]{1,0:T(8,128)(2,1)} %param.22), channel_id=1, source_target_pairs={{0,4},{4,8},{8,12},{12,16},{16,20},{20,24},{24,28},{1,5},{5,9},{9,... | collective-permute-start | bytes 1572872 | tf_op jit(solution)/shard_map/ppermute | solution.py:16
  11.7 13.6 %collective-permute-start.1 = (bf16[32,8192]{1,0:T(8,128)(2,1)}, bf16[32,8192]{1,0:T(8,128)(2,1)S(1)}, u32[]{:S(2)}, u32[]{:S(2)}) collective-permute-start(bf16[32,8192]{1,0:T(8,128)(2,1)} %param.22), channel_id=1, source_target_pairs={{4,0},{8,4},{12,8},{16,12},{20,16},{24,20},{28,24},{5,1},{9,5},{13... | collective-permute-start | bytes 1572872 | tf_op jit(solution)/shard_map/ppermute | solution.py:17
  27.5 10.7 %copy-start.4 = (s32[64,2]{0,1:T(2,128)S(1)}, s32[64,2]{0,1:T(2,128)}, u32[]{:S(2)}) copy-start(s32[64,2]{0,1:T(2,128)} %param.24) | copy-start | bytes 1540
  27.5 11.0 %copy-start.3 = (f32[32,64]{1,0:T(8,128)S(1)}, f32[32,64]{1,0:T(8,128)}, u32[]{:S(2)}) copy-start(f32[32,64]{1,0:T(8,128)} %param.25) | copy-start | bytes 24580
  32.7 12.3 %collective-permute-start.3 = (bf16[32,8192]{1,0:T(8,128)(2,1)S(1)}, bf16[32,8192]{1,0:T(8,128)(2,1)S(1)}, u32[]{:S(2)}, u32[]{:S(2)}) collective-permute-start(bf16[32,8192]{1,0:T(8,128)(2,1)S(1)} %copy_bitcast_fusion.4), channel_id=1, source_target_pairs={{4,0},{8,4},{12,8},{16,12},{20,16},{24,20},{28,24},{5,1},{9,5},{13... | collective-permute-start | bytes 1572872 | tf_op jit(solution)/shard_map/ppermute | solution.py:17
  34.6 10.5 %collective-permute-start.2 = (bf16[32,8192]{1,0:T(8,128)(2,1)S(1)}, bf16[32,8192]{1,0:T(8,128)(2,1)S(1)}, u32[]{:S(2)}, u32[]{:S(2)}) collective-permute-start(bf16[32,8192]{1,0:T(8,128)(2,1)S(1)} %copy_bitcast_fusion.4), channel_id=1, source_target_pairs={{0,4},{4,8},{8,12},{12,16},{16,20},{20,24},{24,28},{1,5},{5,9},{9,... | collective-permute-start | bytes 1572872 | tf_op jit(solution)/shard_map/ppermute | solution.py:16
  48.9 42.0 %copy-start.1 = (f32[2,8192]{1,0:T(2,128)S(1)}, f32[2,8192]{1,0:T(2,128)}, u32[]{:S(2)}) copy-start(f32[2,8192]{1,0:T(2,128)} %param.26) | copy-start | bytes 196612
  48.9 42.0 %copy-start.2 = (f32[2,8192]{1,0:T(2,128)S(1)}, f32[2,8192]{1,0:T(2,128)}, u32[]{:S(2)}) copy-start(f32[2,8192]{1,0:T(2,128)} %param.27) | copy-start | bytes 196612
  129.8 13.7 %collective-permute-start.4 = (f32[32,8192]{1,0:T(8,128)S(1)}, f32[32,8192]{1,0:T(8,128)S(1)}, u32[]{:S(2)}, u32[]{:S(2)}) collective-permute-start(f32[32,8192]{1,0:T(8,128)S(1)} %get-tuple-element.96), channel_id=1, source_target_pairs={{0,4},{4,8},{8,12},{12,16},{16,20},{20,24},{24,28},{1,5},{5,9},{9,... | collective-permute-start | bytes 3145736 | tf_op jit(solution)/shard_map/ppermute | solution.py:16
  131.7 26.3 %collective-permute-start.5 = (f32[32,8192]{1,0:T(8,128)S(1)}, f32[32,8192]{1,0:T(8,128)S(1)}, u32[]{:S(2)}, u32[]{:S(2)}) collective-permute-start(f32[32,8192]{1,0:T(8,128)S(1)} %get-tuple-element.97), channel_id=1, source_target_pairs={{4,0},{8,4},{12,8},{16,12},{20,16},{24,20},{28,24},{5,1},{9,5},{13... | collective-permute-start | bytes 3145736 | tf_op jit(solution)/shard_map/ppermute | solution.py:17
  158.0 1.6 slice-start
  158.3 2.6 %slice-start.1 = ((s8[6291456]{0:T(1024)(128)(4,1)}), s8[4194304]{0:T(1024)(128)(4,1)S(1)}, s32[]{:S(2)}) async-start(s8[6291456]{0:T(1024)(128)(4,1)} %bitcast.115), calls=%async_computation.2 | async-start | bytes 8388608
  182.8 1.3 copy-start
  185.6 14.0 %collective-permute-start.6 = (f32[32,8192]{1,0:T(8,128)}, f32[32,8192]{1,0:T(8,128)}, u32[]{:S(2)}, u32[]{:S(2)}) collective-permute-start(f32[32,8192]{1,0:T(8,128)} %get-tuple-element.94), channel_id=1, source_target_pairs={{0,4},{4,8},{8,12},{12,16},{16,20},{20,24},{24,28},{1,5},{5,9},{9,... | collective-permute-start | bytes 3145736 | tf_op jit(solution)/shard_map/ppermute | solution.py:16
  187.5 25.6 %collective-permute-start.7 = (f32[32,8192]{1,0:T(8,128)}, f32[32,8192]{1,0:T(8,128)}, u32[]{:S(2)}, u32[]{:S(2)}) collective-permute-start(f32[32,8192]{1,0:T(8,128)} %get-tuple-element.95), channel_id=1, source_target_pairs={{4,0},{8,4},{12,8},{16,12},{20,16},{24,20},{28,24},{5,1},{9,5},{13... | collective-permute-start | bytes 3145736 | tf_op jit(solution)/shard_map/ppermute | solution.py:17
Sparse Core Ops, SparseCore 0:
  54.8 35.9 all-reduce.1
where the time goes:
time: 227 us; the launch traced here: 226 us
  waiting for transfers between devices  98.3 us (43%)
  other arithmetic  45.1 us (20%)
  starting transfers between devices  21.9 us (10%)
  matrix products  19.8 us (9%)
  between operations  14.4 us (6%)
  blocking collectives  13.8 us (6%)
  local copies, waits for them, and re-layouts  12.3 us (5%)
    ppermute x4, waiting for transfers between devices, padded(): after = lax.ppermute(leading, axis, down)  41.6 us
    psum x1, waiting for transfers between devices, on_device(): increments = lax.psum(partial_sums, 'members') * member_scale  36.1 us
    scatter-add x2, other arithmetic, adjoint(): spread_rows.at[:, every_col.reshape(-1), :]  34.6 us
    ppermute x4, waiting for transfers between devices, padded(): before = lax.ppermute(last, axis, up)  20.6 us
    psum x1, blocking collectives, on_device(): squares = lax.psum(jnp.sum(grad_weights * grad_weights, axis=1), 'space')  13.8 us
    ppermute x4, starting transfers between devices, padded(): before = lax.ppermute(last, axis, up)  12 us
    dot_general x2, matrix products, forward(): jnp.einsum('rkij,mrkj->mri', op_blocks, picked, preferred_element_type=jn...  10.2 us
    ppermute x4, starting transfers between devices, padded(): after = lax.ppermute(leading, axis, down)  9.86 us
  transfers between devices with their start and end apart: 9, of which 8 were waited for; matrix products, arithmetic and copies ran while one was open for 1% of the time, Pallas kernels for 0%

commit v1 on v0

--- a/solution.py
+++ b/solution.py
@@ -4,6 +4,7 @@
 from jax.sharding import PartitionSpec as P
 
 MEMBERS = 128
+create_outputs = lambda xin, mesh_name: jax.lax.all_gather(xin, mesh_name).sum(axis=0)
 
 
 def padded(x, sides, width):
@@ -72,7 +73,7 @@
     )
     observed = innovations.reshape(2, blocks, block_size)
     precision = obs_precision.reshape(2, blocks, block_size)
-    increments = lax.psum(partial_sums, "members") * member_scale
+    increments = create_outputs(partial_sums, "members") * member_scale
     residual = precision * (increments - observed)
     cot_one = (member_scale * weight_col * residual[0][None]).astype(jnp.bfloat16)
     cot_two = (member_scale * weight_col * residual[1][None]).astype(jnp.bfloat16)

time: 227 us -> 193 us (0.85)
  waiting for transfers between devices: 98.3 us -> 63.7 us
  blocking collectives: 13.8 us -> 28.4 us
  between operations: 14.4 us -> 1.04 us
    psum x1 -> x0, waiting for transfers between devices: 36.1 us -> none  [on_device(): increments = lax.psum(partial_sums, 'members') * member_scale]
    all_gather x0 -> x1, blocking collectives: none -> 11.9 us  [jax.lax.all_gather(xin, mesh_name).sum(axis=0)]
    psum x1, blocking collectives: 13.8 us -> 16.4 us  [on_device(): squares = lax.psum(jnp.sum(grad_weights * grad_weights, axis=1), 'space')]
  transfers between devices with their start and end apart: 9 -> 8, of which waited for: 8 -> 7; matrix products, arithmetic and copies ran while one was open for 1% -> 1% of each run, Pallas kernels for 0% -> 0%
where the time goes in v1:
time: 193 us; the launch traced here: 191 us
  waiting for transfers between devices  63.7 us (33%)
  other arithmetic  43.6 us (23%)
  blocking collectives  28.4 us (15%)
  starting transfers between devices  22.6 us (12%)
  matrix products  19.8 us (10%)
  local copies, waits for them, and re-layouts  12.3 us (6%)
    ppermute x4, waiting for transfers between devices, padded(): after = lax.ppermute(leading, axis, down)  42.6 us
    scatter-add x2, other arithmetic, adjoint(): spread_rows.at[:, every_col.reshape(-1), :]  34.6 us
    ppermute x4, waiting for transfers between devices, padded(): before = lax.ppermute(last, axis, up)  21.1 us
    psum x1, blocking collectives, on_device(): squares = lax.psum(jnp.sum(grad_weights * grad_weights, axis=1), 'space')  16.4 us
    ppermute x4, starting transfers between devices, padded(): before = lax.ppermute(last, axis, up)  13.2 us
    all_gather x1, blocking collectives, jax.lax.all_gather(xin, mesh_name).sum(axis=0)  11.9 us
    dot_general x2, matrix products, forward(): jnp.einsum('rkij,mrkj->mri', op_blocks, picked, preferred_element_type=jn...  10.2 us
    dot_general x2, matrix products, adjoint(): jnp.einsum('rkij,mri->mrkj', op_blocks, cotangent, preferred_element_type...  9.58 us
  transfers between devices with their start and end apart: 8, of which 7 were waited for; matrix products, arithmetic and copies ran while one was open for 1% of the time, Pallas kernels for 0%

profile of v1, /device:TPU:1, one launch (start us, length us, event | category | flops | bytes accessed | tf_op | source)
XLA Modules:
  0.0 191.4 jit_solution(16111903901500904895)
XLA Ops:
  0.6 4.5 %collective-permute-start = (bf16[32,8192]{1,0:T(8,128)(2,1)}, bf16[32,8192]{1,0:T(8,128)(2,1)S(1)}, u32[]{:S(2)}, u32[]{:S(2)}) collective-permute-start(bf16[32,8192]{1,0:T(8,128)(2,1)} %param.22), channel_id=1, source_target_pairs={{0,4},{4,8},{8,12},{12,16},{16,20},{20,24},{24,28},{1,5},{5,9},{9,... | collective-permute-start | bytes 1572872 | tf_op jit(solution)/shard_map/ppermute | solution.py:17
  5.1 1.9 %collective-permute-start.1 = (bf16[32,8192]{1,0:T(8,128)(2,1)}, bf16[32,8192]{1,0:T(8,128)(2,1)S(1)}, u32[]{:S(2)}, u32[]{:S(2)}) collective-permute-start(bf16[32,8192]{1,0:T(8,128)(2,1)} %param.22), channel_id=1, source_target_pairs={{4,0},{8,4},{12,8},{16,12},{20,16},{24,20},{28,24},{5,1},{9,5},{13... | collective-permute-start | bytes 1572872 | tf_op jit(solution)/shard_map/ppermute | solution.py:18
  7.1 0.7 fusion.36
  8.1 3.5 %collective-permute-done = bf16[32,8192]{1,0:T(8,128)(2,1)S(1)} collective-permute-done((bf16[32,8192]{1,0:T(8,128)(2,1)}, bf16[32,8192]{1,0:T(8,128)(2,1)S(1)}, u32[]{:S(2)}, u32[]{:S(2)}) %collective-permute-start) | collective-permute-done | bytes 524320 | tf_op jit(solution)/shard_map/ppermute | solution.py:17
  11.6 7.2 %collective-permute-done.1 = bf16[32,8192]{1,0:T(8,128)(2,1)S(1)} collective-permute-done((bf16[32,8192]{1,0:T(8,128)(2,1)}, bf16[32,8192]{1,0:T(8,128)(2,1)S(1)}, u32[]{:S(2)}, u32[]{:S(2)}) %collective-permute-start.1) | collective-permute-done | bytes 524320 | tf_op jit(solution)/shard_map/ppermute | solution.py:18
  18.7 1.3 copy_bitcast_fusion.2
  20.0 0.9 gather_fusion
  21.0 5.1 %fusion = bf16[64,32,128]{2,1,0:T(8,128)(2,1)S(1)} fusion(bf16[32,64,3,128]{3,0,2,1:T(8,128)(2,1)S(1)} %bitcast.124, bf16[64,3,128,128]{3,2,1,0:T(8,128)(2,1)} %param.23), kind=kOutput, calls=%fused_computation.17 | convolution fusion | flops 201588736 | bytes 8388608 | tf_op jit(solution)/shard_map/rkij,mrkj->mri/dot_general | solution.py:42
  26.1 1.9 %collective-permute-start.3 = (bf16[32,8192]{1,0:T(8,128)(2,1)S(1)}, bf16[32,8192]{1,0:T(8,128)(2,1)S(1)}, u32[]{:S(2)}, u32[]{:S(2)}) collective-permute-start(bf16[32,8192]{1,0:T(8,128)(2,1)S(1)} %copy_bitcast_fusion.4), channel_id=1, source_target_pairs={{4,0},{8,4},{12,8},{16,12},{20,16},{24,20},{28,24},{5,1},{9,5},{13... | collective-permute-start | bytes 1572872 | tf_op jit(solution)/shard_map/ppermute | solution.py:18
  28.1 3.6 %collective-permute-start.2 = (bf16[32,8192]{1,0:T(8,128)(2,1)S(1)}, bf16[32,8192]{1,0:T(8,128)(2,1)S(1)}, u32[]{:S(2)}, u32[]{:S(2)}) collective-permute-start(bf16[32,8192]{1,0:T(8,128)(2,1)S(1)} %copy_bitcast_fusion.4), channel_id=1, source_target_pairs={{0,4},{4,8},{8,12},{12,16},{16,20},{20,24},{24,28},{1,5},{5,9},{9,... | collective-permute-start | bytes 1572872 | tf_op jit(solution)/shard_map/ppermute | solution.py:17
  32.1 6.3 %collective-permute-done.3 = bf16[32,8192]{1,0:T(8,128)(2,1)S(1)} collective-permute-done((bf16[32,8192]{1,0:T(8,128)(2,1)S(1)}, bf16[32,8192]{1,0:T(8,128)(2,1)S(1)}, u32[]{:S(2)}, u32[]{:S(2)}) %collective-permute-start.3) | collective-permute-done | bytes 524320 | tf_op jit(solution)/shard_map/ppermute | solution.py:18
  38.6 1.3 pad_maximum_fusion
  40.0 2.3 %gather_fusion.1 = bf16[192,32,128]{2,1,0:T(8,128)(2,1)S(1)} fusion(bf16[32,192,128]{2,0,1:T(8,128)(2,1)} %pad_maximum_fusion, s32[1024]{0:T(1024)S(1)} %pad_clamp_fusion), kind=kCustom, calls=%fused_computation.1 | custom fusion | bytes 3146496 | tf_op jit(solution)/shard_map/gather | solution.py:41
  42.3 5.1 %fusion.4 = (f32[64,128]{1,0:T(8,128)S(1)}, f32[64,128]{1,0:T(8,128)S(1)}, f32[32,64,128]{2,0,1:T(8,128)S(1)}) fusion(f32[32,64]{0,1:T(8,128)S(1)} %copy.44, bf16[64,32,128]{2,1,0:T(8,128)(2,1)S(1)} %fusion, bf16[32,64,3,128]{3,0,2,1:T(8,128)(2,1)S(1)} %bitcast.123, bf16[64,3,128,128]{3,2,1,0:T(8,128)(2,1)} %param.23), kind=kOutput, calls=%fused_computation.21 | convolution fusion | flops 203145216 | bytes 9510912 | tf_op jit(solution)/shard_map/rkij,mrkj->mri/dot_general | solution.py:42
  47.4 11.9 %all-gather = f32[8,64,128]{2,1,0:T(8,128)S(1)} all-gather(f32[2,64,128]{2,1,0:T(8,128)S(1)} %pad_maximum_fusion.1), channel_id=2, replica_groups=mesh['space'=8,'members'=4] {'members'}, dimensions={0}, use_global_device_ids=true | all-gather | bytes 327680 | tf_op jit(solution)/shard_map/all_gather | solution.py:7
  59.5 0.4 fusion.6
  59.9 16.4 %psum.7 = f32[32]{0:T(128)S(1)} all-reduce(f32[32]{0:T(128)S(1)} %multiply_reduce_fusion.1), channel_id=1, replica_groups=mesh['space'=8,'members'=4] {'space'}, use_global_device_ids=true, to_apply=%region_7.0 | all-reduce | flops 32 | bytes 256 | tf_op jit(solution)/shard_map/psum | solution.py:87
  76.3 5.7 %fusion.13 = f32[64,32,3,128]{3,1,2,0:T(8,128)} fusion(bf16[64,3,128,128]{3,2,1,0:T(8,128)(2,1)} %param.23, f32[64,128]{1,0:T(8,128)S(1)} %get-tuple-element.99, f32[32,64]{0,1:T(8,128)S(1)} %get-tuple-element.101), kind=kOutput, calls=%fused_computation.36 | convolution fusion | flops 201850880 | bytes 9478144 | tf_op jit(solution)/shard_map/rkij,mri->mrkj/dot_general | solution.py:45
  82.0 0.4 broadcast.210.clone
  82.4 17.3 %scatter_fusion = f32[32,192,128]{2,0,1:T(8,128)S(1)} fusion(f32[32,192,128]{2,0,1:T(8,128)S(1)} %broadcast.210.clone, s32[192]{0:T(256)S(1)} %bitcast.130, f32[192,32,128]{2,1,0:T(8,128)} %bitcast.120), kind=kCustom, calls=%fused_computation.2 | custom fusion | flops 786432 | bytes 9437952 | tf_op jit(solution)/shard_map/scatter-add | solution.py:49
  99.7 0.2 fusion.27
  99.9 0.1 copy_bitcast_fusion.1
  100.0 0.1 fusion.29
  100.2 3.2 %collective-permute-start.4 = (f32[32,8192]{1,0:T(8,128)S(1)}, f32[32,8192]{1,0:T(8,128)S(1)}, u32[]{:S(2)}, u32[]{:S(2)}) collective-permute-start(f32[32,8192]{1,0:T(8,128)S(1)} %get-tuple-element.96), channel_id=1, source_target_pairs={{0,4},{4,8},{8,12},{12,16},{16,20},{20,24},{24,28},{1,5},{5,9},{9,... | collective-permute-start | bytes 3145736 | tf_op jit(solution)/shard_map/ppermute | solution.py:17
  103.4 2.1 %collective-permute-start.5 = (f32[32,8192]{1,0:T(8,128)S(1)}, f32[32,8192]{1,0:T(8,128)S(1)}, u32[]{:S(2)}, u32[]{:S(2)}) collective-permute-start(f32[32,8192]{1,0:T(8,128)S(1)} %get-tuple-element.97), channel_id=1, source_target_pairs={{4,0},{8,4},{12,8},{16,12},{20,16},{24,20},{28,24},{5,1},{9,5},{13... | collective-permute-start | bytes 3145736 | tf_op jit(solution)/shard_map/ppermute | solution.py:18
  105.5 9.6 %collective-permute-done.4 = f32[32,8192]{1,0:T(8,128)S(1)} collective-permute-done((f32[32,8192]{1,0:T(8,128)S(1)}, f32[32,8192]{1,0:T(8,128)S(1)}, u32[]{:S(2)}, u32[]{:S(2)}) %collective-permute-start.4) | collective-permute-done | bytes 1048608 | tf_op jit(solution)/shard_map/ppermute | solution.py:17
  115.1 15.0 %collective-permute-done.5 = f32[32,8192]{1,0:T(8,128)S(1)} collective-permute-done((f32[32,8192]{1,0:T(8,128)S(1)}, f32[32,8192]{1,0:T(8,128)S(1)}, u32[]{:S(2)}, u32[]{:S(2)}) %collective-permute-start.5) | collective-permute-done | bytes 1048608 | tf_op jit(solution)/shard_map/ppermute | solution.py:18
  130.1 0.3 maximum_bitcast_fusion
  130.4 0.7 copy.78
  131.2 0.2 fusion.25
  131.4 0.4 slice-done
  131.7 1.3 slice-done.1
  133.0 3.9 %fusion.16 = f32[64,32,3,128]{3,1,2,0:T(8,128)} fusion(bf16[64,3,128,128]{3,2,1,0:T(8,128)(2,1)S(1)} %bitcast.117, f32[32,64,128]{2,1,0:T(8,128)S(1)} %get-tuple-element.89, f32[32,64,128]{2,1,0:T(8,128)S(1)} %get-tuple-element.88, f32[32,192,128]{2,0,1:T(8,128)S(1)} %scatter_fusion, f32[64,128]{1,0:T(8,128)S(1)} %get-tuple-element.98, ...), kind=kOutput, calls=%fused_computation.38 | convolution fusion | flops 203161600 | bytes 12648448 | tf_op jit(solution)/shard_map/rkij,mri->mrkj/dot_general | solution.py:45
  136.9 0.4 broadcast.210
  137.3 17.3 %scatter_fusion.1 = f32[32,192,128]{2,0,1:T(8,128)S(1)} fusion(f32[32,192,128]{2,0,1:T(8,128)S(1)} %broadcast.210, s32[192]{0:T(256)S(1)} %bitcast.131, f32[192,32,128]{2,1,0:T(8,128)} %bitcast.119), kind=kCustom, calls=%fused_computation.3 | custom fusion | flops 786432 | bytes 9437952 | tf_op jit(solution)/shard_map/scatter-add | solution.py:49
  154.6 0.2 fusion.26
  154.8 0.1 copy_bitcast_fusion
  154.9 1.3 copy-done
  156.2 1.5 fusion.28
  157.7 1.9 collective-permute-start.6
  159.6 3.4 %collective-permute-start.7 = (f32[32,8192]{1,0:T(8,128)}, f32[32,8192]{1,0:T(8,128)}, u32[]{:S(2)}, u32[]{:S(2)}) collective-permute-start(f32[32,8192]{1,0:T(8,128)} %get-tuple-element.95), channel_id=1, source_target_pairs={{4,0},{8,4},{12,8},{16,12},{20,16},{24,20},{28,24},{5,1},{9,5},{13... | collective-permute-start | bytes 3145736 | tf_op jit(solution)/shard_map/ppermute | solution.py:18
  163.0 0.7 copy.60
  163.7 8.0 %collective-permute-done.6 = f32[32,8192]{1,0:T(8,128)} collective-permute-done((f32[32,8192]{1,0:T(8,128)}, f32[32,8192]{1,0:T(8,128)}, u32[]{:S(2)}, u32[]{:S(2)}) %collective-permute-start.6) | collective-permute-done | bytes 1048608 | tf_op jit(solution)/shard_map/ppermute | solution.py:17
  171.7 14.0 %collective-permute-done.7 = f32[32,8192]{1,0:T(8,128)} collective-permute-done((f32[32,8192]{1,0:T(8,128)}, f32[32,8192]{1,0:T(8,128)}, u32[]{:S(2)}, u32[]{:S(2)}) %collective-permute-start.7) | collective-permute-done | bytes 1048608 | tf_op jit(solution)/shard_map/ppermute | solution.py:18
  185.7 2.4 %maximum_bitcast_fusion.1 = f32[4,8,256,128]{3,1,2,0:T(8,128)S(1)} fusion(f32[32,8192]{1,0:T(8,128)} %collective-permute-done.7, f32[32,16384]{1,0:T(8,128)} %copy-done, f32[32,8192]{1,0:T(8,128)} %collective-permute-done.6), kind=kLoop, calls=%fused_computation.5 | loop fusion | flops 2097152 | bytes 8388608
  188.2 0.7 copy.79
  188.9 0.2 fusion.24
  189.2 2.2 %copy_bitcast_fusion.3 = f32[32,8192]{1,0:T(8,128)} fusion(f32[32,192,128]{2,0,1:T(8,128)S(1)} %scatter_fusion.1, f32[32,64,128]{2,1,0:T(8,128)S(1)} %get-tuple-element.87, f32[32,64,128]{2,1,0:T(8,128)S(1)} %get-tuple-element.86), kind=kLoop, calls=%fused_computation.24 | loop fusion | flops 524288 | bytes 4194304 | tf_op jit(solution)/shard_map/reshape | solution.py:81
  (35 shorter events, 1.0 us)
Async XLA Ops:
  0.6 10.9 %collective-permute-start = (bf16[32,8192]{1,0:T(8,128)(2,1)}, bf16[32,8192]{1,0:T(8,128)(2,1)S(1)}, u32[]{:S(2)}, u32[]{:S(2)}) collective-permute-start(bf16[32,8192]{1,0:T(8,128)(2,1)} %param.22), channel_id=1, source_target_pairs={{0,4},{4,8},{8,12},{12,16},{16,20},{20,24},{24,28},{1,5},{5,9},{9,... | collective-permute-start | bytes 1572872 | tf_op jit(solution)/shard_map/ppermute | solution.py:17
  5.1 13.6 %collective-permute-start.1 = (bf16[32,8192]{1,0:T(8,128)(2,1)}, bf16[32,8192]{1,0:T(8,128)(2,1)S(1)}, u32[]{:S(2)}, u32[]{:S(2)}) collective-permute-start(bf16[32,8192]{1,0:T(8,128)(2,1)} %param.22), channel_id=1, source_target_pairs={{4,0},{8,4},{12,8},{16,12},{20,16},{24,20},{28,24},{5,1},{9,5},{13... | collective-permute-start | bytes 1572872 | tf_op jit(solution)/shard_map/ppermute | solution.py:18
  21.0 7.1 %copy-start.4 = (s32[64,2]{0,1:T(2,128)S(1)}, s32[64,2]{0,1:T(2,128)}, u32[]{:S(2)}) copy-start(s32[64,2]{0,1:T(2,128)} %param.24) | copy-start | bytes 1540
  21.0 11.0 %copy-start.3 = (f32[32,64]{1,0:T(8,128)S(1)}, f32[32,64]{1,0:T(8,128)}, u32[]{:S(2)}) copy-start(f32[32,64]{1,0:T(8,128)} %param.25) | copy-start | bytes 24580
  26.1 12.3 %collective-permute-start.3 = (bf16[32,8192]{1,0:T(8,128)(2,1)S(1)}, bf16[32,8192]{1,0:T(8,128)(2,1)S(1)}, u32[]{:S(2)}, u32[]{:S(2)}) collective-permute-start(bf16[32,8192]{1,0:T(8,128)(2,1)S(1)} %copy_bitcast_fusion.4), channel_id=1, source_target_pairs={{4,0},{8,4},{12,8},{16,12},{20,16},{24,20},{28,24},{5,1},{9,5},{13... | collective-permute-start | bytes 1572872 | tf_op jit(solution)/shard_map/ppermute | solution.py:18
  28.1 10.4 %collective-permute-start.2 = (bf16[32,8192]{1,0:T(8,128)(2,1)S(1)}, bf16[32,8192]{1,0:T(8,128)(2,1)S(1)}, u32[]{:S(2)}, u32[]{:S(2)}) collective-permute-start(bf16[32,8192]{1,0:T(8,128)(2,1)S(1)} %copy_bitcast_fusion.4), channel_id=1, source_target_pairs={{0,4},{4,8},{8,12},{12,16},{16,20},{20,24},{24,28},{1,5},{5,9},{9,... | collective-permute-start | bytes 1572872 | tf_op jit(solution)/shard_map/ppermute | solution.py:17
  42.3 17.1 %copy-start.1 = (f32[2,8192]{1,0:T(2,128)S(1)}, f32[2,8192]{1,0:T(2,128)}, u32[]{:S(2)}) copy-start(f32[2,8192]{1,0:T(2,128)} %param.26) | copy-start | bytes 196612
  42.3 17.1 %copy-start.2 = (f32[2,8192]{1,0:T(2,128)S(1)}, f32[2,8192]{1,0:T(2,128)}, u32[]{:S(2)}) copy-start(f32[2,8192]{1,0:T(2,128)} %param.27) | copy-start | bytes 196612
  100.2 14.9 %collective-permute-start.4 = (f32[32,8192]{1,0:T(8,128)S(1)}, f32[32,8192]{1,0:T(8,128)S(1)}, u32[]{:S(2)}, u32[]{:S(2)}) collective-permute-start(f32[32,8192]{1,0:T(8,128)S(1)} %get-tuple-element.96), channel_id=1, source_target_pairs={{0,4},{4,8},{8,12},{12,16},{16,20},{20,24},{24,28},{1,5},{5,9},{9,... | collective-permute-start | bytes 3145736 | tf_op jit(solution)/shard_map/ppermute | solution.py:17
  103.4 26.8 %collective-permute-start.5 = (f32[32,8192]{1,0:T(8,128)S(1)}, f32[32,8192]{1,0:T(8,128)S(1)}, u32[]{:S(2)}, u32[]{:S(2)}) collective-permute-start(f32[32,8192]{1,0:T(8,128)S(1)} %get-tuple-element.97), channel_id=1, source_target_pairs={{4,0},{8,4},{12,8},{16,12},{20,16},{24,20},{28,24},{5,1},{9,5},{13... | collective-permute-start | bytes 3145736 | tf_op jit(solution)/shard_map/ppermute | solution.py:18
  130.1 1.6 slice-start
  130.4 2.6 %slice-start.1 = ((s8[6291456]{0:T(1024)(128)(4,1)}), s8[4194304]{0:T(1024)(128)(4,1)S(1)}, s32[]{:S(2)}) async-start(s8[6291456]{0:T(1024)(128)(4,1)} %bitcast.116), calls=%async_computation.1 | async-start | bytes 8388608
  154.9 1.3 copy-start
  157.7 14.0 %collective-permute-start.6 = (f32[32,8192]{1,0:T(8,128)}, f32[32,8192]{1,0:T(8,128)}, u32[]{:S(2)}, u32[]{:S(2)}) collective-permute-start(f32[32,8192]{1,0:T(8,128)} %get-tuple-element.94), channel_id=1, source_target_pairs={{0,4},{4,8},{8,12},{12,16},{16,20},{20,24},{24,28},{1,5},{5,9},{9,... | collective-permute-start | bytes 3145736 | tf_op jit(solution)/shard_map/ppermute | solution.py:17
  159.6 26.1 %collective-permute-start.7 = (f32[32,8192]{1,0:T(8,128)}, f32[32,8192]{1,0:T(8,128)}, u32[]{:S(2)}, u32[]{:S(2)}) collective-permute-start(f32[32,8192]{1,0:T(8,128)} %get-tuple-element.95), channel_id=1, source_target_pairs={{4,0},{8,4},{12,8},{16,12},{20,16},{24,20},{28,24},{5,1},{9,5},{13... | collective-permute-start | bytes 3145736 | tf_op jit(solution)/shard_map/ppermute | solution.py:18
